TPU v7x, 512 devices: a whole 4x8x8 slice. The times are simulated.
512 devices in a mesh: lon: 64 (over x, y_hi, z), lat: 8 (over y_lo, core).
Axes of the slice: x: 4, y: 8 (y_hi: 2, y_lo: 4; y = y_hi * 4 + y_lo), z: 8, core: 2. Of those that a mesh axis runs over, the one named last changes fastest.
Arguments:
- fields: bfloat16 [2048, 512, 256], P('lon', 'lat'), may hold values from -48 to 48
Outputs:
- coarse_fluxes: bfloat16 [2048, 512, 256], P('lon', 'lat')
- snapshot_gram: float32 [64, 64], replicated
All inputs are finite; a program needn't handle non-finite values.
Results may differ from a plain program's by a relative error of at most 0.0064.
Values may be sent and summed in bfloat16 or wider, within the bound.
A program may use at most 64 MiB of HBM per device.

v0:
```python
import jax
import jax.numpy as jnp
from jax import lax
from jax.sharding import Mesh
from jax.sharding import PartitionSpec as P

R = 128
LON = ("lon_0", "lon_1", "lon_2")
LAT = ("lat_0", "lat_1")
LON_LAT = ("lon_0", "lon_1", "lon_2", "lat_0", "lat_1")


def from_behind(shard, axis, by):
    peers = lax.axis_size(axis)
    pairs = [(i, i + by) for i in range(peers) if 0 <= i + by < peers]
    return lax.ppermute(shard, axis, pairs)


def by_axis(shard, axes):
    for axis in axes:
        shard = lax.psum(shard, axis)
    return shard


def tap_block(row_count, col_count, offset):
    row_ids = lax.broadcasted_iota(jnp.int32, (row_count, col_count), 0)
    col_ids = lax.broadcasted_iota(jnp.int32, (row_count, col_count), 1)
    distance = col_ids - row_ids + offset
    weight = jnp.exp(-((distance.astype(jnp.float32) / R) ** 2))
    return jnp.where(jnp.abs(distance) <= R, weight, 0.0).astype(jnp.bfloat16)


def flux_products(values, snapshots):
    left_side = jnp.concatenate([values[:, :, : 3 * snapshots], values[:, :, :snapshots]], axis=2)
    right_side = jnp.concatenate(
        [values[:, :, 3 * snapshots :]] * 3 + [values[:, :, snapshots : 2 * snapshots]], axis=2
    )
    return (left_side.astype(jnp.float32) * right_side.astype(jnp.float32)).astype(jnp.bfloat16)


def shards(fields):
    lon_cells, lat_cells, channels = fields.shape
    snapshots = channels // 4
    total_lon = lon_cells * lax.axis_size(LON)
    total_lat = lat_cells * lax.axis_size(LAT)
    products = flux_products(fields, snapshots)
    flattened = products.reshape(lon_cells, lat_cells * channels)
    lon_norm = jnp.sum(tap_block(1, 2 * R + 1, -R).astype(jnp.float32))
    cycle_rows = lax.all_to_all(flattened, LON, split_axis=1, concat_axis=0, tiled=True)
    blocks = cycle_rows.reshape(total_lon // R, R, cycle_rows.shape[1])
    near_taps = tap_block(R, 3 * R, -R)
    summed = jnp.einsum(
        "ij,bjk->bik", near_taps[:, R : 2 * R], blocks, preferred_element_type=jnp.float32
    )
    summed = summed + jnp.einsum(
        "ij,bjk->bik", near_taps[:, :R], jnp.roll(blocks, 1, 0), preferred_element_type=jnp.float32
    )
    summed = summed + jnp.einsum(
        "ij,bjk->bik",
        near_taps[:, 2 * R :],
        jnp.roll(blocks, -1, 0),
        preferred_element_type=jnp.float32,
    )
    filtered = (summed / lon_norm).astype(jnp.bfloat16).reshape(total_lon, cycle_rows.shape[1])
    lon_done = lax.all_to_all(filtered, LON, split_axis=0, concat_axis=1, tiled=True)
    smoothed = lon_done.reshape(lon_cells, lat_cells, channels)
    row_start = lax.axis_index(LAT) * lat_cells
    lat_weights = tap_block(lat_cells, total_lat, -row_start).astype(jnp.float32)
    lat_norm = jnp.sum(lat_weights, axis=1)
    reach_count = -(-R // lat_cells)
    summed = jnp.einsum(
        "ij,xjc->xic",
        tap_block(lat_cells, lat_cells, 0),
        smoothed,
        preferred_element_type=jnp.float32,
    )
    shift_list = [sign * depth for depth in range(1, reach_count + 1) for sign in (1, -1)]
    for offset_by in shift_list:
        shard_piece = from_behind(smoothed, LAT, offset_by)
        summed = summed + jnp.einsum(
            "ij,xjc->xic",
            tap_block(lat_cells, lat_cells, -offset_by * lat_cells),
            shard_piece,
            preferred_element_type=jnp.float32,
        )
    coarse_fluxes = (summed / lat_norm[None, :, None]).astype(jnp.bfloat16)
    rows_flat = coarse_fluxes.reshape(-1, snapshots)
    partial_gram = lax.dot_general(
        rows_flat, rows_flat, (((0,), (0,)), ((), ())), preferred_element_type=jnp.float32
    )
    snapshot_gram = by_axis(partial_gram, LON_LAT) / (4 * total_lon * total_lat)
    return (coarse_fluxes, snapshot_gram)


def solution(mesh):
    split = Mesh(mesh.devices.reshape(4, 2, 8, 4, 2), ("lon_0", "lon_1", "lon_2", "lat_0", "lat_1"))
    in_specs = (P(LON, LAT, None),)
    out_specs = (P(LON, LAT, None), P())
    return jax.shard_map(
        shards, mesh=split, in_specs=in_specs, out_specs=out_specs, check_vma=False
    )
```

profile of v0, /device:TPU:1, one launch (start us, length us, event | category | flops | bytes accessed | tf_op | source)
XLA Modules:
  0.0 222.7 jit_solution(15256719595227012851)
XLA Ops:
  0.6 1.8 fusion.69
  2.4 0.0 copy-start
  2.4 0.3 copy.26
  2.8 0.3 copy.27
  3.1 0.3 copy.28
  3.5 0.2 copy-done
  3.6 0.6 copy.25
  4.2 2.0 multiply_convert_fusion
  6.2 19.6 %all-to-all-start = ((bf16[32,64,256]{2,0,1:T(8,128)(2,1)}), bf16[32,64,256]{2,0,1:T(8,128)(2,1)S(1)}, u32[]{:S(2)}, u32[]{:S(2)}) async-start(bf16[32,64,256]{2,0,1:T(8,128)(2,1)} %multiply_convert_fusion), calls=%async_computation | async-start | bytes 2097152 | tf_op jit(solution)/shard_map/all_to_all | solution.py:49
  25.8 0.6 fusion.46
  26.5 0.1 select_convert_fusion
  26.5 25.4 %all-to-all-done = bf16[32,64,256]{2,0,1:T(8,128)(2,1)S(1)} async-done(((bf16[32,64,256]{2,0,1:T(8,128)(2,1)}), bf16[32,64,256]{2,0,1:T(8,128)(2,1)S(1)}, u32[]{:S(2)}, u32[]{:S(2)}) %all-to-all-start) | async-done | bytes 1048608 | tf_op jit(solution)/shard_map/all_to_all | solution.py:49
  51.9 0.2 fusion.67
  52.2 0.4 fusion.8
  52.6 0.4 fusion
  53.0 1.1 divide_convert_fusion.1
  54.1 43.6 %all_to_all.29 = bf16[64,32,256]{2,1,0:T(8,128)(2,1)S(1)} all-to-all(bf16[64,32,256]{2,1,0:T(8,128)(2,1)S(1)} %bitcast.55), channel_id=1, replica_groups=mesh['lon_0'=4,'lon_1'=2,'lon_2'=8,'lat_0'=4,'lat_1'=2] {'lon_0','lon_1'..., dimensions={0} | all-to-all | bytes 2097152 | tf_op jit(solution)/shard_map/all_to_all | solution.py:65
  97.8 1.6 copy.31
  99.3 6.6 %collective-permute-start.2 = (bf16[32,64,256]{2,1,0:T(8,128)(2,1)}, bf16[32,64,256]{2,1,0:T(8,128)(2,1)}, u32[]{:S(2)}, u32[]{:S(2)}) collective-permute-start(bf16[32,64,256]{2,1,0:T(8,128)(2,1)} %bitcast.48), channel_id=1, source_target_pairs={{0,2},{1,3},{2,4},{3,5},{4,6},{5,7},{8,10},{9,11},{10,12},{11,13},... | collective-permute-start | bytes 3145736 | tf_op jit(solution)/shard_map/ppermute | solution.py:16
  106.0 3.3 %collective-permute-start.1 = (bf16[32,64,256]{2,1,0:T(8,128)(2,1)}, bf16[32,64,256]{2,1,0:T(8,128)(2,1)S(1)}, u32[]{:S(2)}, u32[]{:S(2)}) collective-permute-start(bf16[32,64,256]{2,1,0:T(8,128)(2,1)} %bitcast.48), channel_id=1, source_target_pairs={{1,0},{2,1},{3,2},{4,3},{5,4},{6,5},{7,6},{9,8},{10,9},{11,10},{12... | collective-permute-start | bytes 3145736 | tf_op jit(solution)/shard_map/ppermute | solution.py:16
  109.3 2.2 collective-permute-start
  111.5 0.2 convert_reduce_fusion
  111.7 1.3 collective-permute-start.3
  113.0 0.9 fusion.20
  113.9 12.7 %collective-permute-done.2 = bf16[32,64,256]{2,1,0:T(8,128)(2,1)} collective-permute-done((bf16[32,64,256]{2,1,0:T(8,128)(2,1)}, bf16[32,64,256]{2,1,0:T(8,128)(2,1)}, u32[]{:S(2)}, u32[]{:S(2)}) %collective-permute-start.2) | collective-permute-done | bytes 1048608 | tf_op jit(solution)/shard_map/ppermute | solution.py:16
  126.6 1.6 fusion.14
  128.3 0.1 collective-permute-done.1
  128.3 0.4 fusion.16
  128.8 10.7 %collective-permute-done = bf16[32,64,256]{2,1,0:T(8,128)(2,1)S(1)} collective-permute-done((bf16[32,64,256]{2,1,0:T(8,128)(2,1)}, bf16[32,64,256]{2,1,0:T(8,128)(2,1)S(1)}, u32[]{:S(2)}, u32[]{:S(2)}) %collective-permute-start) | collective-permute-done | bytes 1048608 | tf_op jit(solution)/shard_map/ppermute | solution.py:16
  139.5 0.4 fusion.18
  139.9 0.0 collective-permute-done.3
  139.9 0.7 fusion.7
  140.6 0.0 copy-start.1
  140.6 0.9 reshape.78
  141.5 0.7 fusion.70
  142.2 0.0 copy-done.1
  142.2 11.6 %psum.35 = f32[64,64]{1,0:T(8,128)S(1)} all-reduce(f32[64,64]{1,0:T(8,128)S(1)} %fusion.70), channel_id=1, replica_groups=mesh['lon_0'=4,'lon_1'=2,'lon_2'=8,'lat_0'=4,'lat_1'=2] {'lon_0'}, use_global_device_ids=true, to_apply=%region_2.3 | all-reduce | flops 4096 | bytes 32768 | tf_op jit(solution)/shard_map/psum | solution.py:21
  153.8 9.1 %psum.36 = f32[64,64]{1,0:T(8,128)S(1)} all-reduce(f32[64,64]{1,0:T(8,128)S(1)} %psum.35), channel_id=1, replica_groups=mesh['lon_0'=4,'lon_1'=2,'lon_2'=8,'lat_0'=4,'lat_1'=2] {'lon_1'}, use_global_device_ids=true, to_apply=%region_3.4 | all-reduce | flops 4096 | bytes 32768 | tf_op jit(solution)/shard_map/psum | solution.py:21
  162.9 22.3 %psum.37 = f32[64,64]{1,0:T(8,128)S(1)} all-reduce(f32[64,64]{1,0:T(8,128)S(1)} %psum.36), channel_id=1, replica_groups=mesh['lon_0'=4,'lon_1'=2,'lon_2'=8,'lat_0'=4,'lat_1'=2] {'lon_2'}, use_global_device_ids=true, to_apply=%region_4.5 | all-reduce | flops 4096 | bytes 32768 | tf_op jit(solution)/shard_map/psum | solution.py:21
  185.3 12.4 %psum.38 = f32[64,64]{1,0:T(8,128)S(1)} all-reduce(f32[64,64]{1,0:T(8,128)S(1)} %psum.37), channel_id=1, replica_groups=mesh['lon_0'=4,'lon_1'=2,'lon_2'=8,'lat_0'=4,'lat_1'=2] {'lat_0'}, use_global_device_ids=true, to_apply=%region_5.6 | all-reduce | flops 4096 | bytes 32768 | tf_op jit(solution)/shard_map/psum | solution.py:21
  197.7 24.4 %psum.39 = f32[64,64]{1,0:T(8,128)S(1)} all-reduce(f32[64,64]{1,0:T(8,128)S(1)} %psum.38), channel_id=1, replica_groups=mesh['lon_0'=4,'lon_1'=2,'lon_2'=8,'lat_0'=4,'lat_1'=2] {'lat_1'}, use_global_device_ids=true, to_apply=%region_6.7 | all-reduce | flops 4096 | bytes 32768 | tf_op jit(solution)/shard_map/psum | solution.py:21
  222.1 0.6 broadcast_multiply_fusion
  (1 shorter events, 0.0 us)
Async XLA Ops:
  2.4 1.2 copy-start
  6.2 45.7 %all-to-all-start = ((bf16[32,64,256]{2,0,1:T(8,128)(2,1)}), bf16[32,64,256]{2,0,1:T(8,128)(2,1)S(1)}, u32[]{:S(2)}, u32[]{:S(2)}) async-start(bf16[32,64,256]{2,0,1:T(8,128)(2,1)} %multiply_convert_fusion), calls=%async_computation | async-start | bytes 2097152 | tf_op jit(solution)/shard_map/all_to_all | solution.py:49
  99.3 27.3 %collective-permute-start.2 = (bf16[32,64,256]{2,1,0:T(8,128)(2,1)}, bf16[32,64,256]{2,1,0:T(8,128)(2,1)}, u32[]{:S(2)}, u32[]{:S(2)}) collective-permute-start(bf16[32,64,256]{2,1,0:T(8,128)(2,1)} %bitcast.48), channel_id=1, source_target_pairs={{0,2},{1,3},{2,4},{3,5},{4,6},{5,7},{8,10},{9,11},{10,12},{11,13},... | collective-permute-start | bytes 3145736 | tf_op jit(solution)/shard_map/ppermute | solution.py:16
  106.0 22.4 %collective-permute-start.1 = (bf16[32,64,256]{2,1,0:T(8,128)(2,1)}, bf16[32,64,256]{2,1,0:T(8,128)(2,1)S(1)}, u32[]{:S(2)}, u32[]{:S(2)}) collective-permute-start(bf16[32,64,256]{2,1,0:T(8,128)(2,1)} %bitcast.48), channel_id=1, source_target_pairs={{1,0},{2,1},{3,2},{4,3},{5,4},{6,5},{7,6},{9,8},{10,9},{11,10},{12... | collective-permute-start | bytes 3145736 | tf_op jit(solution)/shard_map/ppermute | solution.py:16
  109.3 30.2 %collective-permute-start = (bf16[32,64,256]{2,1,0:T(8,128)(2,1)}, bf16[32,64,256]{2,1,0:T(8,128)(2,1)S(1)}, u32[]{:S(2)}, u32[]{:S(2)}) collective-permute-start(bf16[32,64,256]{2,1,0:T(8,128)(2,1)} %bitcast.48), channel_id=1, source_target_pairs={{0,1},{1,2},{2,3},{3,4},{4,5},{5,6},{6,7},{8,9},{9,10},{10,11},{11... | collective-permute-start | bytes 3145736 | tf_op jit(solution)/shard_map/ppermute | solution.py:16
  111.7 28.2 %collective-permute-start.3 = (bf16[32,64,256]{2,1,0:T(8,128)(2,1)}, bf16[32,64,256]{2,1,0:T(8,128)(2,1)S(1)}, u32[]{:S(2)}, u32[]{:S(2)}) collective-permute-start(bf16[32,64,256]{2,1,0:T(8,128)(2,1)} %bitcast.48), channel_id=1, source_target_pairs={{2,0},{3,1},{4,2},{5,3},{6,4},{7,5},{10,8},{11,9},{12,10},{13,11},... | collective-permute-start | bytes 3145736 | tf_op jit(solution)/shard_map/ppermute | solution.py:16
  140.6 1.6 copy-start.1
where the time goes:
time: 223 us
  blocking collectives  123 us (55%)
  waiting for transfers between devices  48.9 us (22%)
  starting transfers between devices  33.1 us (15%)
  matrix products  6.75 us (3%)
  local copies, waits for them, and re-layouts  6.22 us (3%)
  other arithmetic  3.49 us (2%)
    psum x5, blocking collectives, by_axis(): shard = lax.psum(shard, axis)  79.8 us
    all_to_all x1, blocking collectives, shards(): lax.all_to_all(filtered, LON, split_axis=0, concat_axis=1, tiled=True)  43.6 us
    all_to_all x1, waiting for transfers between devices, shards(): lax.all_to_all(flattened, LON, split_axis=1, concat_axis=0, tiled=True)  25.4 us
    ppermute x4, waiting for transfers between devices, from_behind(): return lax.ppermute(shard, axis, pairs)  23.5 us
    all_to_all x1, starting transfers between devices, shards(): lax.all_to_all(flattened, LON, split_axis=1, concat_axis=0, tiled=True)  19.6 us
    ppermute x4, starting transfers between devices, from_behind(): return lax.ppermute(shard, axis, pairs)  13.5 us
  transfers between devices with their start and end apart: 5, of which 4 were waited for; matrix products, arithmetic and copies ran while one was open for 2% of the time, Pallas kernels for 0%

commit v1 on v0

v1 whole, which is shorter than its diff:
```python
import numpy as np
import jax
import jax.numpy as jnp
from jax import lax
from jax.experimental import pallas as pl
from jax.experimental.pallas import tpu as pltpu
from jax.sharding import Mesh
from jax.sharding import PartitionSpec as P

AXES = ("X", "H", "Z", "L", "C")
LON = ("X", "H", "Z")
LAT = ("L", "C")
R = 128
NX, NY, NZ = 4, 8, 8
ROWS, LANES = 16, 128
MESH_ID = pl.DeviceIdType.MESH
F32, BF16 = jnp.float32, jnp.bfloat16
NT = (((1,), (1,)), ((), ()))


def taps(distance):
    weight = jnp.exp(-((distance.astype(F32) / R) ** 2))
    return jnp.where(jnp.abs(distance) <= R, weight, 0.0)


def lon_norm():
    d = np.arange(-R, R + 1).astype(np.float32)
    return float(np.sum(np.exp(-((d / R) ** 2)).astype(BF16).astype(np.float32)))


def iota(shape, axis):
    return lax.broadcasted_iota(jnp.int32, shape, axis)


def identity(n):
    return jnp.where(iota((n, n), 0) == iota((n, n), 1), 1.0, 0.0).astype(BF16)


def kernel(
    fields, out, gram,
    T, SA, SB, R1A, R1B, R2A, R2B, HA, HB, XO, XH, SM, AO, AH, W, OA, OB, Q1A, Q1B, FA, FB, MB, GA,
    g_part, g_core, g_z, g_y, g_x, g_end,
    loc, a1s, b1s, a1r, b1r, a2s, b2s, a2r, b2r, hs, hr, a3s, b3s, a3r, b3r, a4s, b4s, a4r, b4r, gs, gr,
):
    x, h, z = lax.axis_index("X"), lax.axis_index("H"), lax.axis_index("Z")
    l, c = lax.axis_index("L"), lax.axis_index("C")
    y = h * 4 + l
    yc = y * 2 + c

    def at_z(d):
        return {"Z": (z + d) % NZ}

    def at_yc(dy, dc):
        yy = (y + dy) % NY
        return {"H": yy // 4, "L": yy % 4, "C": (c + dc) % 2}

    def send(src, dst, ssem, rsem, device):
        pltpu.make_async_remote_copy(src, dst, ssem, rsem, device_id=device, device_id_type=MESH_ID).start()

    def wait(ref, sem):
        pltpu.make_async_copy(ref, ref, sem).wait()

    def local(src, dst, k):
        copy = pltpu.make_async_copy(src, dst, loc.at[k])
        copy.start()
        return copy

    z_offsets = [1, 7, 6, 5, 4, 3, 2]
    yc_offsets = [(dy, dc) for dy in (1, 7, 6, 5, 4, 3, 2, 0) for dc in (0, 1) if (dy, dc) != (0, 0)]

    barrier = pltpu.get_barrier_semaphore()
    for d in z_offsets:
        pl.semaphore_signal(barrier, inc=1, device_id=at_z(d), device_id_type=MESH_ID)
    for dy, dc in yc_offsets:
        pl.semaphore_signal(barrier, inc=1, device_id=at_yc(dy, dc), device_id_type=MESH_ID)
    for d in (1, 2, 3):
        pl.semaphore_signal(barrier, inc=1, device_id={"X": (x + d) % NX}, device_id_type=MESH_ID)

    eye = identity(256)

    def to_channels(t, carry):
        cells = fields[pl.ds(t * 2, 2)].reshape(128, 256)
        f = lax.dot_general(eye, cells, NT, preferred_element_type=F32)
        u, v, w, b = f[0:64], f[64:128], f[128:192], f[192:256]
        base = pl.multiple_of(t * 256, 256)
        T[pl.ds(base, 64), :] = u * b
        T[pl.ds(base + 64, 64), :] = v * b
        T[pl.ds(base + 128, 64), :] = w * b
        T[pl.ds(base + 192, 64), :] = u * v
        return carry

    lax.fori_loop(0, 16, to_channels, 0)

    def pack(k, carry):
        for j in range(8):
            ch = k * 8 + j
            SA[ch] = T[pl.ds(ch, 16, stride=256), :].astype(BF16)
            SB[ch] = T[pl.ds(ch + 128, 16, stride=256), :].astype(BF16)
        return carry

    lax.fori_loop(0, 16, pack, 0)
    pl.semaphore_wait(barrier, 25)

    for d in z_offsets:
        i = (1 - d) % 8
        send(SA.at[pl.ds(((z + d) % NZ) * 16, 16)], R1A.at[i], a1s, a1r.at[i // 4], at_z(d))
    own_a1 = local(SA.at[pl.ds(z * 16, 16)], R1A.at[1], 0)
    for dy, dc in yc_offsets:
        i = (1 - dy) % 8
        to = ((y + dy) % NY) * 2 + (c + dc) % 2
        send(SB.at[pl.ds(to * 8, 8)], R1B.at[2 * i + c], b1s, b1r.at[i // 4], at_yc(dy, dc))
    own_b1 = local(SB.at[pl.ds(yc * 8, 8)], R1B.at[2 + c], 1)

    def lon_matrix(k, carry):
        for block, shift in ((0, 0), (1, -1), (2, 1)):
            row = iota((32, 256), 0) + k * 32
            AO[pl.ds(block * 256 + k * 32, 32), :] = taps(2 * (iota((32, 256), 1) - row) + shift).astype(BF16)
            col = iota((32, 128), 1)
            col = jnp.where(col < 64, col - 64, col + 192)
            row = iota((32, 128), 0) + k * 32
            AH[pl.ds(block * 256 + k * 32, 32), :] = taps(2 * (col - row) + shift).astype(BF16)
        return carry

    lax.fori_loop(0, 8, lon_matrix, 0)

    def lat_matrix(k, carry):
        src = iota((32, 256), 0) + k * 32
        dst = iota((32, 256), 1)
        same = (src // 64) % 2 == (dst // 64) % 2
        apart = 64 * (src // 128 - dst // 128) + src % 64 - dst % 64
        for step in range(3):
            W[step, pl.ds(k * 32, 32), :] = jnp.where(same, taps(apart - 128 * (step - 1)), 0.0).astype(BF16)
        return carry

    lax.fori_loop(0, 8, lat_matrix, 0)
    ones = jnp.ones((16, 256), BF16)
    lat_sums = [jnp.dot(ones, W[k], preferred_element_type=F32)[0:1] for k in range(3)]
    inv_lat = []
    for dst in range(4):
        total = lat_sums[1]
        if dst > 0:
            total = total + lat_sums[2]
        if dst < 3:
            total = total + lat_sums[0]
        inv_lat.append(1.0 / total)
    inv_lon = 1.0 / lon_norm()

    own2 = []
    for g in (0, 1):
        if g == 0:
            own_a1.wait()
            wait(R1A.at[pl.ds(0, 3)], a1r.at[0])
        else:
            wait(R1A.at[pl.ds(0, 4)], a1r.at[1])
        for dy, dc in yc_offsets:
            to = ((y + dy) % NY) * 2 + (c + dc) % 2
            send(R1A.at[pl.ds(4 * g, 4), to], R2A.at[yc, pl.ds(4 * g, 4)], a2s, a2r.at[g], at_yc(dy, dc))
        own2.append(local(R1A.at[pl.ds(4 * g, 4), yc], R2A.at[yc, pl.ds(4 * g, 4)], 2 + g))
        if g == 0:
            own_b1.wait()
            wait(R1B.at[pl.ds(0, 7)], b1r.at[0])
        else:
            wait(R1B.at[pl.ds(0, 8)], b1r.at[1])
        for d in z_offsets:
            send(R1B.at[pl.ds(8 * g, 8), (z + d) % NZ], R2B.at[z, pl.ds(8 * g, 8)], b2s, b2r.at[g], at_z(d))
        own2.append(local(R1B.at[pl.ds(8 * g, 8), z], R2B.at[z, pl.ds(8 * g, 8)], 4 + g))

    for g in (0, 1):
        own2[2 * g].wait()
        wait(R2A.at[pl.ds(0, 15), pl.ds(0, 4)], a2r.at[g])
        for i in range(4 * g, 4 * g + 4):
            zz = (z + i + 7) % NZ
            hi = zz // 4
            send(R2A.at[pl.ds(hi * 8, 8), i], HA.at[hi, zz % 4], hs.at[0], hr.at[0], {"X": (x + 2 * hi + 3) % NX})
        own2[2 * g + 1].wait()
        wait(R2B.at[pl.ds(0, 7), pl.ds(0, 8)], b2r.at[g])
        for i in range(4 * g, 4 * g + 4):
            yy = (y + i + 7) % NY
            hi = yy // 4
            send(
                R2B.at[pl.ds(hi * 4, 4), pl.ds(2 * i, 2)],
                HB.at[hi, :, pl.ds((yy % 4) * 2, 2)],
                hs.at[1], hr.at[1], {"X": (x + 2 * hi + 3) % NX},
            )

    def filtered(tile_of, halo, halo_sem, store):
        def gather(lam, carry):
            for mu in range(8):
                XO[pl.ds(pl.multiple_of(lam * 16, 16), 16), mu * 128 : mu * 128 + 128] = tile_of(lam, mu)
            return carry

        lax.fori_loop(0, 16, gather, 0)
        wait(halo, halo_sem)
        for hi in (0, 1):
            for zz in range(4):
                for mu in range(8):
                    row = (1 - hi) * 64 + zz * 16
                    XH[row : row + 16, mu * 128 : mu * 128 + 128] = halo[hi, zz, mu]
        first = iota((256, 128), 1) < 64
        for n in range(8):
            cols = slice(n * 128, n * 128 + 128)
            if n % 2 == 0:
                wide = slice(n * 128, n * 128 + 256)
                zs = jnp.dot(AO[...], XO[:, wide], preferred_element_type=F32)
                zs = zs + jnp.dot(AH[...], XH[:, wide], preferred_element_type=F32)
            part = zs[:, (n % 2) * 128 : (n % 2) * 128 + 128]
            other = jnp.where(first, part[256:512], part[512:768])
            total = part[0:256] + pltpu.roll(other, 64, 1)
            SM[:, cols] = (total * inv_lon).astype(BF16)
        for dst in range(4):
            total = None
            for src in range(max(0, dst - 1), min(3, dst + 1) + 1):
                term = jnp.dot(SM[:, src * 256 : src * 256 + 256], W[dst - src + 1], preferred_element_type=F32)
                total = term if total is None else total + term
            total = (total * inv_lat[dst]).astype(BF16)
            for lam in range(16):
                for half in range(2):
                    store(lam, 2 * dst + half, total[lam * 16 : lam * 16 + 16, half * 128 : half * 128 + 128])

    def store_a(lam, mu, tile):
        OA[(lam // 8) * 8 + mu, (lam % 8 - z + 9) % NZ] = tile

    def store_b(lam, mu, tile):
        OB[lam % 8, 2 * (((lam // 8) * 4 + mu // 2 - y + 9) % NY) + mu % 2] = tile

    filtered(lambda lam, mu: R2A[(lam // 8) * 8 + mu, (lam % 8 - z + 9) % NZ], HA, hr.at[0], store_a)
    own3 = {}
    for g in (1, 0):
        for dy, dc in yc_offsets:
            to = ((y + dy) % NY) * 2 + (c + dc) % 2
            send(OA.at[to, pl.ds(4 * g, 4)], Q1A.at[yc, pl.ds(4 * g, 4)], a3s, a3r.at[g], at_yc(dy, dc))
        own3["a", g] = local(OA.at[yc, pl.ds(4 * g, 4)], Q1A.at[yc, pl.ds(4 * g, 4)], 6 + g)
    filtered(
        lambda lam, mu: R2B[lam % 8, 2 * (((lam // 8) * 4 + mu // 2 - y + 9) % NY) + mu % 2], HB, hr.at[1], store_b
    )
    for g in (1, 0):
        for d in z_offsets:
            send(OB.at[(z + d) % NZ, pl.ds(8 * g, 8)], Q1B.at[z, pl.ds(8 * g, 8)], b3s, b3r.at[g], at_z(d))
        own3["b", g] = local(OB.at[z, pl.ds(8 * g, 8)], Q1B.at[z, pl.ds(8 * g, 8)], 8 + g)

    own4 = []
    for g in (1, 0):
        own3["a", g].wait()
        wait(Q1A.at[pl.ds(0, 15), pl.ds(0, 4)], a3r.at[g])
        for k in range(4 * g, 4 * g + 4):
            d = (k - 1) % 8
            if d:
                send(Q1A.at[:, k], FA.at[pl.ds(z * 16, 16)], a4s, a4r, at_z(d))
            else:
                own4.append(local(Q1A.at[:, k], FA.at[pl.ds(z * 16, 16)], 10))
        own3["b", g].wait()
        wait(Q1B.at[pl.ds(0, 7), pl.ds(0, 8)], b3r.at[g])
        for k in range(4 * g, 4 * g + 4):
            dy = (k - 1) % 8
            for dc in (0, 1):
                kc = 2 * k + (c + dc) % 2
                if dy or dc:
                    send(Q1B.at[:, kc], FB.at[pl.ds(yc * 8, 8)], b4s, b4r, at_yc(dy, dc))
                else:
                    own4.append(local(Q1B.at[:, kc], FB.at[pl.ds(yc * 8, 8)], 11))

    def unpack_of(src, first_row):
        def unpack(k, carry):
            for j in range(8):
                ch = k * 8 + j
                T[pl.ds(ch + first_row, 16, stride=256), :] = src[ch].astype(F32)
            return carry

        return unpack

    for copy in own4:
        copy.wait()
    wait(FA.at[pl.ds(0, 112)], a4r)
    lax.fori_loop(0, 16, unpack_of(FA, 0), 0)
    wait(FB.at[pl.ds(0, 120)], b4r)
    lax.fori_loop(0, 16, unpack_of(FB, 128), 0)

    GA[...] = jnp.zeros_like(GA)

    def gram_term(t, carry):
        m = T[pl.ds(pl.multiple_of(t * 256, 256), 256), :].astype(BF16)
        MB[t] = m
        GA[...] += lax.dot_general(m, m, NT, preferred_element_type=F32)
        return carry

    lax.fori_loop(0, 16, gram_term, 0)

    left = GA[0:64, 0:128] + GA[128:192, 128:256]
    right = GA[64:128, 0:128] + GA[192:256, 128:256]
    g64 = left + pltpu.roll(right, 64, 1)
    low = iota((32, 128), 1) < 64
    g_part[...] = jnp.where(low, g64[0:32], pltpu.roll(g64[32:64], 64, 1))
    other_core = {"C": 1 - c}
    send(g_part.at[pl.ds((1 - c) * 16, 16)], g_core, gs.at[0], gr.at[0], other_core)
    wait(g_core, gr.at[0])
    g_z[z] = g_part[pl.ds(pl.multiple_of(c * 16, 16), 16), :] + g_core[...]
    for d in z_offsets:
        send(g_z.at[z], g_z.at[z], gs.at[1], gr.at[1], at_z(d))

    eye_cells = identity(128)

    def to_cells(t, carry):
        cells = lax.dot_general(eye_cells, MB[t], NT, preferred_element_type=F32)
        out[pl.ds(t * 2, 2)] = cells.astype(BF16).reshape(2, 64, 256)
        return carry

    lax.fori_loop(0, 16, to_cells, 0)

    wait(g_z.at[pl.ds(0, 7)], gr.at[1])
    total = g_z[0]
    for k in range(1, NZ):
        total = total + g_z[k]
    g_y[y] = total
    for d in (1, 7, 2, 6, 3, 5, 4):
        send(g_y.at[y], g_y.at[y], gs.at[2], gr.at[2], at_yc(d, 0))
    wait(g_y.at[pl.ds(0, 7)], gr.at[2])
    total = g_y[0]
    for k in range(1, NY):
        total = total + g_y[k]
    g_x[x] = total
    for d in (1, 2, 3):
        send(g_x.at[x], g_x.at[x], gs.at[3], gr.at[3], {"X": (x + d) % NX})
    wait(g_x.at[pl.ds(0, 3)], gr.at[3])
    total = g_x[0]
    for k in range(1, NX):
        total = total + g_x[k]
    g_end[c] = total * (1.0 / (4 * 2048 * 512))
    send(g_end.at[c], g_end.at[c], gs.at[4], gr.at[4], other_core)
    wait(g_end.at[0], gr.at[4])
    gram[0:16, :] = g_end[0, :, 0:64]
    gram[16:32, :] = g_end[1, :, 0:64]
    gram[32:48, :] = pltpu.roll(g_end[0], 64, 1)[:, 0:64]
    gram[48:64, :] = pltpu.roll(g_end[1], 64, 1)[:, 0:64]

    wait(SA.at[pl.ds(0, 112)], a1s)
    wait(SB.at[pl.ds(0, 120)], b1s)
    wait(R2A.at[pl.ds(0, 15)], a2s)
    wait(R2B.at[pl.ds(0, 7)], b2s)
    wait(HA, hs.at[0])
    wait(HB, hs.at[1])
    wait(OA.at[pl.ds(0, 15)], a3s)
    wait(OB.at[pl.ds(0, 7)], b3s)
    wait(FA.at[pl.ds(0, 112)], a4s)
    wait(FB.at[pl.ds(0, 120)], b4s)
    wait(g_core, gs.at[0])
    wait(g_z.at[pl.ds(0, 7)], gs.at[1])
    wait(g_y.at[pl.ds(0, 7)], gs.at[2])
    wait(g_x.at[pl.ds(0, 3)], gs.at[3])
    wait(g_end.at[0], gs.at[4])


def tiles(*lead):
    return pltpu.VMEM(lead + (ROWS, LANES), BF16)


def shards(fields):
    vmem, dma = pltpu.VMEM, pltpu.SemaphoreType.DMA
    scratch = [
        vmem((4096, 128), F32),
        tiles(128), tiles(128),
        tiles(8, 16), tiles(16, 8),
        tiles(16, 8), tiles(8, 16),
        tiles(2, 4, 8), tiles(2, 4, 8),
        vmem((256, 1024), BF16), vmem((128, 1024), BF16), vmem((256, 1024), BF16),
        vmem((768, 256), BF16), vmem((768, 128), BF16), vmem((3, 256, 256), BF16),
        tiles(16, 8), tiles(8, 16),
        tiles(16, 8), tiles(8, 16),
        tiles(128), tiles(128),
        vmem((16, 256, 128), BF16), vmem((256, 256), F32),
        vmem((32, 128), F32), vmem((16, 128), F32),
        vmem((8, 16, 128), F32), vmem((8, 16, 128), F32), vmem((4, 16, 128), F32), vmem((2, 16, 128), F32),
        dma((12,)),
        dma(()), dma(()), dma((2,)), dma((2,)),
        dma(()), dma(()), dma((2,)), dma((2,)),
        dma((2,)), dma((2,)),
        dma(()), dma(()), dma((2,)), dma((2,)),
        dma(()), dma(()), dma(()), dma(()),
        dma((5,)), dma((5,)),
    ]
    return pl.pallas_call(
        kernel,
        name="coarse_grain",
        out_shape=(
            jax.ShapeDtypeStruct((32, 64, 256), BF16),
            jax.ShapeDtypeStruct((64, 64), F32),
        ),
        in_specs=[pl.BlockSpec(memory_space=pltpu.VMEM)],
        out_specs=(pl.BlockSpec(memory_space=pltpu.VMEM), pl.BlockSpec(memory_space=pltpu.VMEM)),
        scratch_shapes=scratch,
        compiler_params=pltpu.CompilerParams(
            collective_id=0, has_side_effects=True, vmem_limit_bytes=40 << 20
        ),
    )(fields)


def solution(mesh):
    split = Mesh(mesh.devices.reshape(4, 2, 8, 4, 2), AXES)
    return jax.shard_map(
        shards, mesh=split, in_specs=(P(LON, LAT, None),), out_specs=(P(LON, LAT, None), P()), check_vma=False
    )
```

time: 223 us -> 97.9 us (0.44)
  blocking collectives: 123 us -> 0 us
  Pallas kernels: 0 us -> 94.3 us
  waiting for transfers between devices: 48.9 us -> 0 us
  starting transfers between devices: 33.1 us -> 0 us
  matrix products: 6.75 us -> 0 us
  other arithmetic: 3.49 us -> 0 us
  local copies, waits for them, and re-layouts: 6.22 us -> 2.8 us
    pallas_call x0 -> x1, Pallas kernels: none -> 94.3 us  [shards(): pl.pallas_call(kernel, name='coarse_grain', out_shape=(jax.ShapeDtypeStru...]
    psum x5 -> x0, blocking collectives: 79.8 us -> none  [by_axis(): shard = lax.psum(shard, axis)]
    all_to_all x1 -> x0, blocking collectives: 43.6 us -> none  [shards(): lax.all_to_all(filtered, LON, split_axis=0, concat_axis=1, tiled=True)]
    all_to_all x1 -> x0, waiting for transfers between devices: 25.4 us -> none  [shards(): lax.all_to_all(flattened, LON, split_axis=1, concat_axis=0, tiled=True)]
    ppermute x4 -> x0, waiting for transfers between devices: 23.5 us -> none  [from_behind(): return lax.ppermute(shard, axis, pairs)]
    all_to_all x1 -> x0, starting transfers between devices: 19.6 us -> none  [shards(): lax.all_to_all(flattened, LON, split_axis=1, concat_axis=0, tiled=True)]
    ppermute x4 -> x0, starting transfers between devices: 13.5 us -> none  [from_behind(): return lax.ppermute(shard, axis, pairs)]
    dot_general x9 -> x0, matrix products: 6.75 us -> none  [the longest x4 3.2 us: shards(): jnp.einsum('ij,xjc->xic', tap_block(lat_cells, lat_cells, -offset_by * la...]
  transfers between devices with their start and end apart: 5 -> 0, of which waited for: 4 -> 0; matrix products, arithmetic and copies ran while one was open for 2% -> 0% of each run, Pallas kernels for 0% -> 0%
where the time goes in v1:
time: 97.9 us; the launch traced here: 97.8 us
  Pallas kernels  94.3 us (96%)
  local copies, waits for them, and re-layouts  2.8 us (3%)
    pallas_call x1, Pallas kernels, shards(): pl.pallas_call(kernel, name='coarse_grain', out_shape=(jax.ShapeDtypeStru...  94.3 us
    unnamed x4, local copies, waits for them, and re-layouts  2.8 us

profile of v1, /device:TPU:1, one launch (start us, length us, event | category | flops | bytes accessed | tf_op | source)
XLA Modules:
  0.0 97.8 jit_solution(2940424105962833211)
XLA Ops:
  0.6 0.0 copy-start
  0.6 1.2 %copy-done = bf16[32,64,256]{2,1,0:T(8,128)(2,1)S(1)} copy-done((bf16[32,64,256]{2,1,0:T(8,128)(2,1)S(1)}, bf16[32,64,256]{2,1,0:T(8,128)(2,1)}, u32[]{:S(2)}) %copy-start) | copy-done | bytes 1048600
  1.9 94.3 %coarse_grain.1 = (bf16[32,64,256]{2,1,0:T(8,128)(2,1)S(1)}, f32[64,64]{1,0:T(8,128)S(1)}) custom-call(bf16[32,64,256]{2,1,0:T(8,128)(2,1)S(1)} %copy-done), custom_call_target="tpu_custom_call" | custom-call | tf_op jit(solution)/shard_map/coarse_grain/pallas_call | solution.py:380
  96.2 1.0 copy.5
  97.2 0.6 copy.6
Async XLA Ops:
  0.6 1.2 %copy-start = (bf16[32,64,256]{2,1,0:T(8,128)(2,1)S(1)}, bf16[32,64,256]{2,1,0:T(8,128)(2,1)}, u32[]{:S(2)}) copy-start(bf16[32,64,256]{2,1,0:T(8,128)(2,1)} %fields.1) | copy-start | bytes 3145732

commit v2 on v1

v2 whole, which is shorter than its diff:
```python
import numpy as np
import jax
import jax.numpy as jnp
from jax import lax
from jax.experimental import pallas as pl
from jax.experimental.pallas import tpu as pltpu
from jax.sharding import Mesh
from jax.sharding import PartitionSpec as P

AXES = ("X", "H", "Z", "L", "C")
LON = ("X", "H", "Z")
LAT = ("L", "C")
R = 128
NX, NY, NZ = 4, 8, 8
ROWS, LANES = 16, 128
MESH_ID = pl.DeviceIdType.MESH
F32, BF16 = jnp.float32, jnp.bfloat16
NT = (((1,), (1,)), ((), ()))


def taps(distance):
    weight = jnp.exp(-((distance.astype(F32) / R) ** 2))
    return jnp.where(jnp.abs(distance) <= R, weight, 0.0)


def lon_norm():
    d = np.arange(-R, R + 1).astype(np.float32)
    return float(np.sum(np.exp(-((d / R) ** 2)).astype(BF16).astype(np.float32)))


def iota(shape, axis):
    return lax.broadcasted_iota(jnp.int32, shape, axis)


def kernel(
    fields, out, gram,
    FV, T, SA, SB, R1A, R1B, R2A, R2B, HA, HB, XA, XB, XH, SM, AO, AH, W, OA, OB, Q1A, Q1B, FA, FB, MW, GA,
    g_part, g_core, g_z, g_y, g_x,
    ins, loc, a1s, b1s, a1r, b1r, a2s, b2s, a2r, b2r, hs, hr, a3s, b3s, a3r, b3r, a4s, b4s, a4r, b4r, gs, gr,
):
    x, h, z = lax.axis_index("X"), lax.axis_index("H"), lax.axis_index("Z")
    l, c = lax.axis_index("L"), lax.axis_index("C")
    y = h * 4 + l
    yc = y * 2 + c

    def at_z(d):
        return {"Z": (z + d) % NZ}

    def at_yc(dy, dc):
        yy = (y + dy) % NY
        return {"H": yy // 4, "L": yy % 4, "C": (c + dc) % 2}

    def at_xc(dx, dc):
        return {"X": (x + dx) % NX, "C": (c + dc) % 2}

    def send(src, dst, ssem, rsem, device):
        pltpu.make_async_remote_copy(src, dst, ssem, rsem, device_id=device, device_id_type=MESH_ID).start()

    def wait(ref, sem):
        pltpu.make_async_copy(ref, ref, sem).wait()

    def local(src, dst, k):
        copy = pltpu.make_async_copy(src, dst, loc.at[k])
        copy.start()
        return copy

    z_near = [1, 7, 6, 5, 4, 3, 2]
    z_far = [4, 3, 5, 2, 6, 1, 7]
    yc_near = [(dy, dc) for dy in (1, 7, 6, 5, 4, 3, 2, 0) for dc in (0, 1) if (dy, dc) != (0, 0)]
    yc_far = [(dy, dc) for dy in (4, 3, 5, 2, 6, 1, 7, 0) for dc in (0, 1) if (dy, dc) != (0, 0)]
    xc_far = [(2, 0), (2, 1), (1, 0), (3, 0), (1, 1), (3, 1), (0, 1)]

    pieces = []
    for k in range(4):
        pieces.append(pltpu.make_async_copy(fields.at[pl.ds(8 * k, 8)], FV.at[pl.ds(8 * k, 8)], ins.at[k]))
        pieces[k].start()

    barrier = pltpu.get_barrier_semaphore()
    for d in z_far:
        pl.semaphore_signal(barrier, inc=1, device_id=at_z(d), device_id_type=MESH_ID)
    for dy, dc in yc_far:
        pl.semaphore_signal(barrier, inc=1, device_id=at_yc(dy, dc), device_id_type=MESH_ID)
    for dx, dc in xc_far[:6]:
        pl.semaphore_signal(barrier, inc=1, device_id=at_xc(dx, dc), device_id_type=MESH_ID)

    def to_channels(t, carry):
        f = jnp.transpose(FV[pl.ds(t * 2, 2)].reshape(128, 256)).astype(F32)
        u, v, w, b = f[0:64], f[64:128], f[128:192], f[192:256]
        base = pl.multiple_of(t * 256, 256)
        T[pl.ds(base, 64), :] = u * b
        T[pl.ds(base + 64, 64), :] = v * b
        T[pl.ds(base + 128, 64), :] = w * b
        T[pl.ds(base + 192, 64), :] = u * v
        return carry

    for k in range(4):
        pieces[k].wait()
        lax.fori_loop(4 * k, 4 * k + 4, to_channels, 0, unroll=4)

    def pack_of(dst, first_row):
        def pack(k, carry):
            for j in range(8):
                ch = k * 8 + j
                dst[ch] = T[pl.ds(ch + first_row, 16, stride=256), :].astype(BF16)
            return carry

        return pack

    lax.fori_loop(0, 16, pack_of(SA, 0), 0)
    pl.semaphore_wait(barrier, 28)
    for d in z_near:
        i = (1 - d) % 8
        send(SA.at[pl.ds(((z + d) % NZ) * 16, 16)], R1A.at[i], a1s, a1r.at[i // 4], at_z(d))
    own_a1 = local(SA.at[pl.ds(z * 16, 16)], R1A.at[1], 0)
    lax.fori_loop(0, 16, pack_of(SB, 128), 0)
    for dy, dc in yc_near:
        i = (1 - dy) % 8
        to = ((y + dy) % NY) * 2 + (c + dc) % 2
        send(SB.at[pl.ds(to * 8, 8)], R1B.at[2 * i + c], b1s, b1r.at[i // 4], at_yc(dy, dc))
    own_b1 = local(SB.at[pl.ds(yc * 8, 8)], R1B.at[2 + c], 1)

    def lon_matrix(k, carry):
        edge = k // 4
        for block, shift in ((0, 0), (1, -1), (2, 1)):
            row = iota((32, 256), 0) + (k % 4) * 32
            row = row + (1 - edge) * 64 + edge * 128 * (row // 64)
            base = pl.multiple_of(edge * 384 + block * 128 + (k % 4) * 32, 32)
            AO[pl.ds(base, 32), :] = taps(2 * (iota((32, 256), 1) - row) + shift).astype(BF16)
        return carry

    lax.fori_loop(0, 8, lon_matrix, 0)

    def halo_matrix(k, carry):
        for block, shift in ((0, 0), (1, -1), (2, 1)):
            row = iota((32, 128), 0) + k * 32
            row = row + 128 * (row // 64)
            col = iota((32, 128), 1)
            col = jnp.where(col < 64, col - 64, col + 192)
            base = pl.multiple_of(block * 128 + k * 32, 32)
            AH[pl.ds(base, 32), :] = taps(2 * (col - row) + shift).astype(BF16)
        return carry

    lax.fori_loop(0, 4, halo_matrix, 0)

    def lat_matrix(k, carry):
        src = iota((32, 256), 0) + k * 32
        dst = iota((32, 256), 1)
        same = (src // 64) % 2 == (dst // 64) % 2
        apart = 64 * (src // 128 - dst // 128) + src % 64 - dst % 64
        for step in range(3):
            W[step, pl.ds(k * 32, 32), :] = jnp.where(same, taps(apart - 128 * (step - 1)), 0.0).astype(BF16)
        return carry

    lax.fori_loop(0, 8, lat_matrix, 0)
    ones = jnp.ones((16, 256), BF16)
    lat_sums = [jnp.dot(ones, W[k], preferred_element_type=F32)[0:1] for k in range(3)]
    inv_lat = []
    for dst in range(4):
        total = lat_sums[1]
        if dst > 0:
            total = total + lat_sums[2]
        if dst < 3:
            total = total + lat_sums[0]
        inv_lat.append(1.0 / total)
    inv_lon = 1.0 / lon_norm()

    own2 = []
    for g in (0, 1):
        if g == 0:
            own_a1.wait()
            wait(R1A.at[pl.ds(0, 3)], a1r.at[0])
        else:
            wait(R1A.at[pl.ds(0, 4)], a1r.at[1])
        for dy, dc in yc_far:
            to = ((y + dy) % NY) * 2 + (c + dc) % 2
            send(R1A.at[pl.ds(4 * g, 4), to], R2A.at[yc, pl.ds(4 * g, 4)], a2s, a2r.at[g], at_yc(dy, dc))
        own2.append(local(R1A.at[pl.ds(4 * g, 4), yc], R2A.at[yc, pl.ds(4 * g, 4)], 2 + g))
        if g == 0:
            own_b1.wait()
            wait(R1B.at[pl.ds(0, 7)], b1r.at[0])
        else:
            wait(R1B.at[pl.ds(0, 8)], b1r.at[1])
        for d in z_far:
            send(R1B.at[pl.ds(8 * g, 8), (z + d) % NZ], R2B.at[z, pl.ds(8 * g, 8)], b2s, b2r.at[g], at_z(d))
        own2.append(local(R1B.at[pl.ds(8 * g, 8), z], R2B.at[z, pl.ds(8 * g, 8)], 4 + g))

    def halo_a(g):
        own2[2 * g].wait()
        wait(R2A.at[pl.ds(0, 15), pl.ds(0, 4)], a2r.at[g])
        for i in range(4 * g, 4 * g + 4):
            zz = (z + i + 7) % NZ
            hi = zz // 4
            send(R2A.at[pl.ds(hi * 8, 8), i], HA.at[hi, zz % 4], hs.at[0], hr.at[0], at_xc(2 * hi + 3, 0))

    def halo_b(g):
        own2[2 * g + 1].wait()
        wait(R2B.at[pl.ds(0, 7), pl.ds(0, 8)], b2r.at[g])
        for i in range(4 * g, 4 * g + 4):
            yy = (y + i + 7) % NY
            hi = yy // 4
            send(
                R2B.at[pl.ds(hi * 4, 4), pl.ds(2 * i, 2)],
                HB.at[hi, :, pl.ds((yy % 4) * 2, 2)],
                hs.at[1], hr.at[1], at_xc(2 * hi + 3, 0),
            )

    def gather(tile_of, X):
        def rows(lam, carry):
            for mu in range(8):
                X[pl.ds(pl.multiple_of(lam * 16, 16), 16), mu * 128 : mu * 128 + 128] = tile_of(lam, mu)
            return carry

        lax.fori_loop(0, 16, rows, 0)

    def gather_halo(halo):
        for hi in (0, 1):
            for zz in range(4):
                for mu in range(8):
                    row = (1 - hi) * 64 + zz * 16
                    XH[row : row + 16, mu * 128 : mu * 128 + 128] = halo[hi, zz, mu]

    def filtered(X, edge, store):
        first = iota((128, 128), 1) < 64
        lams = [0, 1, 2, 3, 12, 13, 14, 15] if edge else list(range(4, 12))
        for n in range(4):
            cols = slice(n * 256, n * 256 + 256)
            zs = jnp.dot(AO[edge * 384 : edge * 384 + 384], X[:, cols], preferred_element_type=F32)
            if edge:
                zs = zs + jnp.dot(AH[...], XH[:, cols], preferred_element_type=F32)
            for half in range(2):
                part = zs[:, half * 128 : half * 128 + 128]
                other = jnp.where(first, part[128:256], part[256:384])
                total = part[0:128] + pltpu.roll(other, 64, 1)
                at = n * 256 + half * 128
                SM[:, at : at + 128] = (total * inv_lon).astype(BF16)
        for dst in range(4):
            total = None
            for src in range(max(0, dst - 1), min(3, dst + 1) + 1):
                term = jnp.dot(SM[:, src * 256 : src * 256 + 256], W[dst - src + 1], preferred_element_type=F32)
                total = term if total is None else total + term
            total = (total * inv_lat[dst]).astype(BF16)
            for k, lam in enumerate(lams):
                for half in range(2):
                    store(lam, 2 * dst + half, total[k * 16 : k * 16 + 16, half * 128 : half * 128 + 128])

    def store_a(lam, mu, tile):
        OA[(lam // 8) * 8 + mu, lam % 8] = tile

    def store_b(lam, mu, tile):
        OB[lam % 8, (lam // 8) * 8 + mu] = tile

    def send_a(edge):
        for dy, dc in yc_far:
            yy = (y + dy) % NY
            to = yy * 2 + (c + dc) % 2
            at = 4 * (yy // 4) if edge else 4 - 4 * (yy // 4)
            send(OA.at[to, pl.ds(at, 4)], Q1A.at[yc, pl.ds(at, 4)], a3s, a3r.at[edge], at_yc(dy, dc))
        at = 4 * h if edge else 4 - 4 * h
        return local(OA.at[yc, pl.ds(at, 4)], Q1A.at[yc, pl.ds(at, 4)], 6 + edge)

    def send_b(edge):
        for d in z_far:
            zz = (z + d) % NZ
            at = 8 * (zz // 4) if edge else 8 - 8 * (zz // 4)
            send(OB.at[zz, pl.ds(at, 8)], Q1B.at[z, pl.ds(at, 8)], b3s, b3r.at[edge], at_z(d))
        at = 8 * (z // 4) if edge else 8 - 8 * (z // 4)
        return local(OB.at[z, pl.ds(at, 8)], Q1B.at[z, pl.ds(at, 8)], 8 + edge)

    halo_a(0)
    halo_b(0)
    halo_a(1)
    gather(lambda lam, mu: R2A[(lam // 8) * 8 + mu, (lam % 8 - z + 9) % NZ], XA)
    filtered(XA, 0, store_a)
    own3 = [send_a(0)]
    halo_b(1)
    gather(lambda lam, mu: R2B[lam % 8, 2 * (((lam // 8) * 4 + mu // 2 - y + 9) % NY) + mu % 2], XB)
    filtered(XB, 0, store_b)
    own3.append(send_b(0))
    wait(HA, hr.at[0])
    gather_halo(HA)
    filtered(XA, 1, store_a)
    own3.append(send_a(1))
    wait(HB, hr.at[1])
    gather_halo(HB)
    filtered(XB, 1, store_b)
    own3.append(send_b(1))

    own3[0].wait()
    own3[2].wait()
    for edge in (0, 1):
        wait(Q1A.at[pl.ds(0, 15), pl.ds(0, 4)], a3r.at[edge])
    for d in z_far:
        send(Q1A.at[:, (z + d) % NZ], FA.at[pl.ds(z * 16, 16)], a4s, a4r, at_z(d))
    own_a4 = local(Q1A.at[:, z], FA.at[pl.ds(z * 16, 16)], 10)
    own3[1].wait()
    own3[3].wait()
    for edge in (0, 1):
        wait(Q1B.at[pl.ds(0, 7), pl.ds(0, 8)], b3r.at[edge])
    for dy, dc in yc_far:
        to = ((y + dy) % NY) * 2 + (c + dc) % 2
        send(Q1B.at[:, to], FB.at[pl.ds(yc * 8, 8)], b4s, b4r, at_yc(dy, dc))
    own_b4 = local(Q1B.at[:, yc], FB.at[pl.ds(yc * 8, 8)], 11)

    def home(src, first_row):
        def unpack(k, carry):
            for j in range(8):
                ch = k * 8 + j
                T[pl.ds(ch + first_row, 16, stride=256), :] = src[ch].astype(F32)
            return carry

        lax.fori_loop(0, 16, unpack, 0)
        rows = slice(first_row, first_row + 128)
        for t in range(16):
            at = t * 256 + first_row
            MW[rows, t * 128 : t * 128 + 128] = T[at : at + 128, :].astype(BF16)
        GA[rows] = lax.dot_general(MW[rows], MW[rows], NT, preferred_element_type=F32)

    own_a4.wait()
    wait(FA.at[pl.ds(0, 112)], a4r)
    home(FA, 0)
    own_b4.wait()
    wait(FB.at[pl.ds(0, 120)], b4r)
    home(FB, 128)

    left = GA[0:64] + GA[128:192]
    right = GA[64:128] + GA[192:256]
    g64 = left + pltpu.roll(right, 64, 1)
    low = iota((32, 128), 1) < 64
    g_part[...] = jnp.where(low, g64[0:32], pltpu.roll(g64[32:64], 64, 1))
    send(g_part.at[pl.ds((1 - c) * 16, 16)], g_core, gs.at[0], gr.at[0], at_yc(0, 1))
    wait(g_core, gr.at[0])
    g_z[z] = g_part[pl.ds(pl.multiple_of(c * 16, 16), 16), :] + g_core[...]
    for d in z_far:
        send(g_z.at[z], g_z.at[z], gs.at[1], gr.at[1], at_z(d))

    def to_cells(t, carry):
        cells = jnp.transpose(MW[:, pl.ds(pl.multiple_of(t * 128, 128), 128)])
        FV[pl.ds(t * 2, 2)] = cells.reshape(2, 64, 256)
        return carry

    lax.fori_loop(0, 16, to_cells, 0, unroll=4)
    finished = pltpu.make_async_copy(FV, out, ins.at[0])
    finished.start()

    wait(g_z.at[pl.ds(0, 7)], gr.at[1])
    total = g_z[0]
    for k in range(1, NZ):
        total = total + g_z[k]
    g_y[y] = total
    for d in z_far:
        send(g_y.at[y], g_y.at[y], gs.at[2], gr.at[2], at_yc(d, 0))
    wait(g_y.at[pl.ds(0, 7)], gr.at[2])
    total = g_y[0]
    for k in range(1, NY):
        total = total + g_y[k]
    g_x[c, x] = total * (1.0 / (4 * 2048 * 512))
    for dx, dc in xc_far:
        send(g_x.at[c, x], g_x.at[c, x], gs.at[3], gr.at[3], at_xc(dx, dc))
    wait(g_y.at[pl.ds(0, 7)], gr.at[3])
    for half in range(2):
        total = g_x[half, 0]
        for k in range(1, NX):
            total = total + g_x[half, k]
        gram[half * 16 : half * 16 + 16, :] = total[:, 0:64]
        gram[32 + half * 16 : 48 + half * 16, :] = pltpu.roll(total, 64, 1)[:, 0:64]

    finished.wait()
    wait(SA.at[pl.ds(0, 112)], a1s)
    wait(SB.at[pl.ds(0, 120)], b1s)
    wait(R2A.at[pl.ds(0, 15)], a2s)
    wait(R2B.at[pl.ds(0, 7)], b2s)
    wait(HA, hs.at[0])
    wait(HB, hs.at[1])
    wait(OA.at[pl.ds(0, 15)], a3s)
    wait(OB.at[pl.ds(0, 7)], b3s)
    wait(FA.at[pl.ds(0, 112)], a4s)
    wait(FB.at[pl.ds(0, 120)], b4s)
    wait(g_core, gs.at[0])
    for k in (1, 2, 3):
        wait(g_z.at[pl.ds(0, 7)], gs.at[k])


def tiles(*lead):
    return pltpu.VMEM(lead + (ROWS, LANES), BF16)


def shards(fields):
    vmem, dma = pltpu.VMEM, pltpu.SemaphoreType.DMA
    scratch = [
        vmem((32, 64, 256), BF16),
        vmem((4096, 128), F32),
        tiles(128), tiles(128),
        tiles(8, 16), tiles(16, 8),
        tiles(16, 8), tiles(8, 16),
        tiles(2, 4, 8), tiles(2, 4, 8),
        vmem((256, 1024), BF16), vmem((256, 1024), BF16), vmem((128, 1024), BF16), vmem((128, 1024), BF16),
        vmem((768, 256), BF16), vmem((384, 128), BF16), vmem((3, 256, 256), BF16),
        tiles(16, 8), tiles(8, 16),
        tiles(16, 8), tiles(8, 16),
        tiles(128), tiles(128),
        vmem((256, 2048), BF16), vmem((256, 128), F32),
        vmem((32, 128), F32), vmem((16, 128), F32),
        vmem((8, 16, 128), F32), vmem((8, 16, 128), F32), vmem((2, 4, 16, 128), F32),
        dma((4,)), dma((12,)),
        dma(()), dma(()), dma((2,)), dma((2,)),
        dma(()), dma(()), dma((2,)), dma((2,)),
        dma((2,)), dma((2,)),
        dma(()), dma(()), dma((2,)), dma((2,)),
        dma(()), dma(()), dma(()), dma(()),
        dma((4,)), dma((4,)),
    ]
    return pl.pallas_call(
        kernel,
        name="coarse_grain",
        out_shape=(
            jax.ShapeDtypeStruct((32, 64, 256), BF16),
            jax.ShapeDtypeStruct((64, 64), F32),
        ),
        in_specs=[pl.BlockSpec(memory_space=pltpu.HBM)],
        out_specs=(pl.BlockSpec(memory_space=pltpu.HBM), pl.BlockSpec(memory_space=pltpu.VMEM)),
        scratch_shapes=scratch,
        compiler_params=pltpu.CompilerParams(
            collective_id=0, has_side_effects=True, vmem_limit_bytes=56_000_000
        ),
    )(fields)


def solution(mesh):
    split = Mesh(mesh.devices.reshape(4, 2, 8, 4, 2), AXES)
    return jax.shard_map(
        shards, mesh=split, in_specs=(P(LON, LAT, None),), out_specs=(P(LON, LAT, None), P()), check_vma=False
    )
```

time: 97.9 us -> 90.7 us (0.926)
  Pallas kernels: 94.3 us -> 87 us
    pallas_call x1, Pallas kernels: 94.3 us -> 87 us  [shards(): pl.pallas_call(kernel, name='coarse_grain', out_shape=(jax.ShapeDtypeStru...]
    unnamed x4 -> x2, local copies, waits for them, and re-layouts: 2.8 us -> 2.92 us
where the time goes in v2:
time: 90.7 us; the launch traced here: 90.5 us
  Pallas kernels  87 us (96%)
  local copies, waits for them, and re-layouts  2.92 us (3%)
    pallas_call x1, Pallas kernels, shards(): pl.pallas_call(kernel, name='coarse_grain', out_shape=(jax.ShapeDtypeStru...  87 us
    unnamed x2, local copies, waits for them, and re-layouts  2.92 us

profile of v2, /device:TPU:1, one launch (start us, length us, event | category | flops | bytes accessed | tf_op | source)
XLA Modules:
  0.0 90.5 jit_solution(14858022122109176062)
XLA Ops:
  0.6 87.0 %coarse_grain.1 = (bf16[32,64,256]{2,1,0:T(8,128)(2,1)}, f32[64,64]{1,0:T(8,128)S(1)}) custom-call(bf16[32,64,256]{2,1,0:T(8,128)(2,1)} %fields.1), custom_call_target="tpu_custom_call" | custom-call | tf_op jit(solution)/shard_map/coarse_grain/pallas_call | solution.py:412
  87.6 2.3 %copy.5 = bf16[32,64,256]{2,1,0:T(8,128)(2,1)} copy(bf16[32,64,256]{2,1,0:T(8,128)(2,1)} %get-tuple-element.4) | data formatting | bytes 2097152
  89.9 0.6 copy.6

commit v3 on v2

--- a/solution.py
+++ b/solution.py
@@ -204,13 +204,22 @@
                 hs.at[1], hr.at[1], at_xc(2 * hi + 3, 0),
             )
 
-    def gather(tile_of, X):
-        def rows(lam, carry):
-            for mu in range(8):
-                X[pl.ds(pl.multiple_of(lam * 16, 16), 16), mu * 128 : mu * 128 + 128] = tile_of(lam, mu)
-            return carry
-
-        lax.fori_loop(0, 16, rows, 0)
+    def gather_a(g):
+        for i in range(4 * g, 4 * g + 4):
+            zz = (z + i + 7) % NZ
+            for hh in (0, 1):
+                row = pl.multiple_of((8 * hh + zz) * 16, 16)
+                for mu in range(8):
+                    XA[pl.ds(row, 16), mu * 128 : mu * 128 + 128] = R2A[8 * hh + mu, i]
+
+    def gather_b(g):
+        for i in range(4 * g, 4 * g + 4):
+            yy = (y + i + 7) % NY
+            for zz in range(8):
+                row = pl.multiple_of((8 * (yy // 4) + zz) * 16, 16)
+                for core in (0, 1):
+                    col = pl.multiple_of((2 * (yy % 4) + core) * 128, 128)
+                    XB[pl.ds(row, 16), pl.ds(col, 128)] = R2B[zz, 2 * i + core]
 
     def gather_halo(halo):
         for hi in (0, 1):
@@ -249,78 +258,106 @@
     def store_b(lam, mu, tile):
         OB[lam % 8, (lam // 8) * 8 + mu] = tile
 
-    def send_a(edge):
+    def part_of(high, part, unit):
+        return 4 * unit * (1 - high) if part == 0 else 4 * unit * high + 2 * unit * (part - 1)
+
+    def send_a(part):
+        n = 2 if part else 4
         for dy, dc in yc_far:
             yy = (y + dy) % NY
             to = yy * 2 + (c + dc) % 2
-            at = 4 * (yy // 4) if edge else 4 - 4 * (yy // 4)
-            send(OA.at[to, pl.ds(at, 4)], Q1A.at[yc, pl.ds(at, 4)], a3s, a3r.at[edge], at_yc(dy, dc))
-        at = 4 * h if edge else 4 - 4 * h
-        return local(OA.at[yc, pl.ds(at, 4)], Q1A.at[yc, pl.ds(at, 4)], 6 + edge)
-
-    def send_b(edge):
+            at = pl.ds(part_of(yy // 4, part, 1), n)
+            send(OA.at[to, at], Q1A.at[yc, at], a3s, a3r.at[part], at_yc(dy, dc))
+        at = pl.ds(part_of(h, part, 1), n)
+        return local(OA.at[yc, at], Q1A.at[yc, at], 6 + part)
+
+    def send_b(part):
+        n = 4 if part else 8
         for d in z_far:
             zz = (z + d) % NZ
-            at = 8 * (zz // 4) if edge else 8 - 8 * (zz // 4)
-            send(OB.at[zz, pl.ds(at, 8)], Q1B.at[z, pl.ds(at, 8)], b3s, b3r.at[edge], at_z(d))
-        at = 8 * (z // 4) if edge else 8 - 8 * (z // 4)
-        return local(OB.at[z, pl.ds(at, 8)], Q1B.at[z, pl.ds(at, 8)], 8 + edge)
+            at = pl.ds(part_of(zz // 4, part, 2), n)
+            send(OB.at[zz, at], Q1B.at[z, at], b3s, b3r.at[part], at_z(d))
+        at = pl.ds(part_of(z // 4, part, 2), n)
+        return local(OB.at[z, at], Q1B.at[z, at], 9 + part)
 
     halo_a(0)
     halo_b(0)
+    gather_a(0)
+    gather_b(0)
     halo_a(1)
-    gather(lambda lam, mu: R2A[(lam // 8) * 8 + mu, (lam % 8 - z + 9) % NZ], XA)
+    gather_a(1)
     filtered(XA, 0, store_a)
     own3 = [send_a(0)]
     halo_b(1)
-    gather(lambda lam, mu: R2B[lam % 8, 2 * (((lam // 8) * 4 + mu // 2 - y + 9) % NY) + mu % 2], XB)
+    gather_b(1)
     filtered(XB, 0, store_b)
     own3.append(send_b(0))
     wait(HA, hr.at[0])
     gather_halo(HA)
     filtered(XA, 1, store_a)
     own3.append(send_a(1))
+    own3.append(send_a(2))
     wait(HB, hr.at[1])
     gather_halo(HB)
     filtered(XB, 1, store_b)
     own3.append(send_b(1))
-
-    own3[0].wait()
-    own3[2].wait()
-    for edge in (0, 1):
-        wait(Q1A.at[pl.ds(0, 15), pl.ds(0, 4)], a3r.at[edge])
-    for d in z_far:
-        send(Q1A.at[:, (z + d) % NZ], FA.at[pl.ds(z * 16, 16)], a4s, a4r, at_z(d))
-    own_a4 = local(Q1A.at[:, z], FA.at[pl.ds(z * 16, 16)], 10)
-    own3[1].wait()
-    own3[3].wait()
-    for edge in (0, 1):
-        wait(Q1B.at[pl.ds(0, 7), pl.ds(0, 8)], b3r.at[edge])
-    for dy, dc in yc_far:
-        to = ((y + dy) % NY) * 2 + (c + dc) % 2
-        send(Q1B.at[:, to], FB.at[pl.ds(yc * 8, 8)], b4s, b4r, at_yc(dy, dc))
-    own_b4 = local(Q1B.at[:, yc], FB.at[pl.ds(yc * 8, 8)], 11)
-
-    def home(src, first_row):
-        def unpack(k, carry):
-            for j in range(8):
-                ch = k * 8 + j
-                T[pl.ds(ch + first_row, 16, stride=256), :] = src[ch].astype(F32)
-            return carry
-
-        lax.fori_loop(0, 16, unpack, 0)
-        rows = slice(first_row, first_row + 128)
+    own3.append(send_b(2))
+
+    for part, ka, kb in ((0, 0, 1), (1, 2, 4), (2, 3, 5)):
+        n = 2 if part else 4
+        own3[ka].wait()
+        wait(Q1A.at[pl.ds(0, 15), pl.ds(0, n)], a3r.at[part])
+        for k in range(n):
+            zz = part_of(h, part, 1) + (z + k) % n
+
+            @pl.when(zz != z)
+            def _():
+                there = (zz - z + NZ) % NZ
+                send(Q1A.at[:, zz], FA.at[pl.ds(z * 16, 16)], a4s, a4r.at[there], {"Z": zz})
+
+        own3[kb].wait()
+        wait(Q1B.at[pl.ds(0, 7), pl.ds(0, 2 * n)], b3r.at[part])
+        for k in range(n):
+            yy = part_of(z // 4, part, 1) + (y + k) % n
+            there = (yy - y + NY) % NY
+            for dc in (1, 0):
+                cc = (c + dc) % 2
+
+                def send_home():
+                    send(
+                        Q1B.at[:, yy * 2 + cc], FB.at[pl.ds(yc * 8, 8)], b4s, b4r.at[there],
+                        {"H": yy // 4, "L": yy % 4, "C": cc},
+                    )
+
+                if dc:
+                    send_home()
+                else:
+                    pl.when(yy != y)(send_home)
+
+    own_a4 = local(Q1A.at[:, z], FA.at[pl.ds(z * 16, 16)], 12)
+    own_b4 = local(Q1B.at[:, yc], FB.at[pl.ds(yc * 8, 8)], 13)
+
+    def home(src, ch, row):
+        for j in range(16):
+            T[pl.ds(row + j, 16, stride=256), :] = src[ch + j].astype(F32)
+        row = pl.multiple_of(row, 16)
         for t in range(16):
-            at = t * 256 + first_row
-            MW[rows, t * 128 : t * 128 + 128] = T[at : at + 128, :].astype(BF16)
+            MW[pl.ds(row, 16), t * 128 : t * 128 + 128] = T[pl.ds(t * 256 + row, 16), :].astype(BF16)
+
+    own_a4.wait()
+    home(FA, z * 16, z * 16)
+    own_b4.wait()
+    wait(FB.at[pl.ds(0, 8)], b4r.at[0])
+    home(FB, y * 16, 128 + y * 16)
+    for d in (1, 7, 2, 6, 3, 5, 4):
+        wait(FA.at[pl.ds(0, 16)], a4r.at[d])
+        zz = (z - d + NZ) % NZ
+        home(FA, zz * 16, zz * 16)
+        wait(FB.at[pl.ds(0, 16)], b4r.at[d])
+        yy = (y - d + NY) % NY
+        home(FB, yy * 16, 128 + yy * 16)
+    for rows in (slice(0, 128), slice(128, 256)):
         GA[rows] = lax.dot_general(MW[rows], MW[rows], NT, preferred_element_type=F32)
-
-    own_a4.wait()
-    wait(FA.at[pl.ds(0, 112)], a4r)
-    home(FA, 0)
-    own_b4.wait()
-    wait(FB.at[pl.ds(0, 120)], b4r)
-    home(FB, 128)
 
     left = GA[0:64] + GA[128:192]
     right = GA[64:128] + GA[192:256]
@@ -335,12 +372,10 @@
 
     def to_cells(t, carry):
         cells = jnp.transpose(MW[:, pl.ds(pl.multiple_of(t * 128, 128), 128)])
-        FV[pl.ds(t * 2, 2)] = cells.reshape(2, 64, 256)
+        out[pl.ds(t * 2, 2)] = cells.reshape(2, 64, 256)
         return carry
 
     lax.fori_loop(0, 16, to_cells, 0, unroll=4)
-    finished = pltpu.make_async_copy(FV, out, ins.at[0])
-    finished.start()
 
     wait(g_z.at[pl.ds(0, 7)], gr.at[1])
     total = g_z[0]
@@ -364,7 +399,6 @@
         gram[half * 16 : half * 16 + 16, :] = total[:, 0:64]
         gram[32 + half * 16 : 48 + half * 16, :] = pltpu.roll(total, 64, 1)[:, 0:64]
 
-    finished.wait()
     wait(SA.at[pl.ds(0, 112)], a1s)
     wait(SB.at[pl.ds(0, 120)], b1s)
     wait(R2A.at[pl.ds(0, 15)], a2s)
@@ -378,6 +412,17 @@
     wait(g_core, gs.at[0])
     for k in (1, 2, 3):
         wait(g_z.at[pl.ds(0, 7)], gs.at[k])
+
+
+def put_out(coarse, gram, coarse_out, gram_out, sems):
+    copies = [pltpu.make_async_copy(gram, gram_out, sems.at[4])]
+    for k in range(4):
+        part = pl.ds(8 * k, 8)
+        copies.append(pltpu.make_async_copy(coarse.at[part], coarse_out.at[part], sems.at[k]))
+    for copy in copies:
+        copy.start()
+    for copy in copies:
+        copy.wait()
 
 
 def tiles(*lead):
@@ -401,15 +446,15 @@
         vmem((256, 2048), BF16), vmem((256, 128), F32),
         vmem((32, 128), F32), vmem((16, 128), F32),
         vmem((8, 16, 128), F32), vmem((8, 16, 128), F32), vmem((2, 4, 16, 128), F32),
-        dma((4,)), dma((12,)),
+        dma((4,)), dma((14,)),
         dma(()), dma(()), dma((2,)), dma((2,)),
         dma(()), dma(()), dma((2,)), dma((2,)),
         dma((2,)), dma((2,)),
-        dma(()), dma(()), dma((2,)), dma((2,)),
-        dma(()), dma(()), dma(()), dma(()),
+        dma(()), dma(()), dma((3,)), dma((3,)),
+        dma(()), dma(()), dma((8,)), dma((8,)),
         dma((4,)), dma((4,)),
     ]
-    return pl.pallas_call(
+    coarse, gram = pl.pallas_call(
         kernel,
         name="coarse_grain",
         out_shape=(
@@ -417,12 +462,24 @@
             jax.ShapeDtypeStruct((64, 64), F32),
         ),
         in_specs=[pl.BlockSpec(memory_space=pltpu.HBM)],
-        out_specs=(pl.BlockSpec(memory_space=pltpu.HBM), pl.BlockSpec(memory_space=pltpu.VMEM)),
+        out_specs=(pl.BlockSpec(memory_space=pltpu.VMEM), pl.BlockSpec(memory_space=pltpu.VMEM)),
         scratch_shapes=scratch,
         compiler_params=pltpu.CompilerParams(
-            collective_id=0, has_side_effects=True, vmem_limit_bytes=56_000_000
+            collective_id=0, has_side_effects=True, vmem_limit_bytes=55_000_000
         ),
     )(fields)
+    return pl.pallas_call(
+        put_out,
+        name="put_out",
+        out_shape=(
+            jax.ShapeDtypeStruct((32, 64, 256), BF16),
+            jax.ShapeDtypeStruct((64, 64), F32),
+        ),
+        in_specs=[pl.BlockSpec(memory_space=pltpu.VMEM)] * 2,
+        out_specs=(pl.BlockSpec(memory_space=pl.ANY), pl.BlockSpec(memory_space=pl.ANY)),
+        scratch_shapes=[dma((5,))],
+        compiler_params=pltpu.CompilerParams(vmem_limit_bytes=8 << 20),
+    )(coarse, gram)
 
 
 def solution(mesh):

time: 90.7 us -> 86.6 us (0.955)
  local copies, waits for them, and re-layouts: 2.92 us -> 0 us
  Pallas kernels: 87 us -> 85.9 us
    unnamed x2 -> x0, local copies, waits for them, and re-layouts: 2.92 us -> none
    pallas_call x1, Pallas kernels: 87 us -> 84.8 us  [shards(): pl.pallas_call(kernel, name='coarse_grain', out_shape=(jax.ShapeDtypeStru...]
    pallas_call x0 -> x1, Pallas kernels: none -> 1.02 us  [shards(): pl.pallas_call(put_out, name='put_out', out_shape=(jax.ShapeDtypeStruct((...]
where the time goes in v3:
time: 86.6 us; the launch traced here: 86.5 us
  Pallas kernels  85.9 us (99%)
    pallas_call x1, Pallas kernels, shards(): pl.pallas_call(kernel, name='coarse_grain', out_shape=(jax.ShapeDtypeStru...  84.8 us

profile of v3, /device:TPU:1, one launch (start us, length us, event | category | flops | bytes accessed | tf_op | source)
XLA Modules:
  0.0 86.5 jit_solution(14723549226468500733)
XLA Ops:
  0.6 84.8 %coarse_grain.1 = (bf16[32,64,256]{2,1,0:T(8,128)(2,1)S(1)}, f32[64,64]{1,0:T(8,128)S(1)}) custom-call(bf16[32,64,256]{2,1,0:T(8,128)(2,1)} %fields.1), custom_call_target="tpu_custom_call" | custom-call | tf_op jit(solution)/shard_map/coarse_grain/pallas_call | solution.py:457
  85.5 1.0 %put_out.1 = (bf16[32,64,256]{2,1,0:T(8,128)(2,1)}, f32[64,64]{1,0:T(8,128)}) custom-call(bf16[32,64,256]{2,1,0:T(8,128)(2,1)S(1)} %get-tuple-element.4.coarse, f32[64,64]{1,0:T(8,128)S(1)} %get-tuple-element.5.gram), custom_call_target="tpu_custom_call" | custom-call | tf_op jit(solution)/shard_map/put_out/pallas_call | solution.py:471

commit v4 on v3

--- a/solution.py
+++ b/solution.py
@@ -106,18 +106,18 @@
 
         return pack
 
-    lax.fori_loop(0, 16, pack_of(SA, 0), 0)
+    lax.fori_loop(0, 16, pack_of(SB, 128), 0)
     pl.semaphore_wait(barrier, 28)
-    for d in z_near:
-        i = (1 - d) % 8
-        send(SA.at[pl.ds(((z + d) % NZ) * 16, 16)], R1A.at[i], a1s, a1r.at[i // 4], at_z(d))
-    own_a1 = local(SA.at[pl.ds(z * 16, 16)], R1A.at[1], 0)
-    lax.fori_loop(0, 16, pack_of(SB, 128), 0)
     for dy, dc in yc_near:
         i = (1 - dy) % 8
         to = ((y + dy) % NY) * 2 + (c + dc) % 2
         send(SB.at[pl.ds(to * 8, 8)], R1B.at[2 * i + c], b1s, b1r.at[i // 4], at_yc(dy, dc))
     own_b1 = local(SB.at[pl.ds(yc * 8, 8)], R1B.at[2 + c], 1)
+    lax.fori_loop(0, 16, pack_of(SA, 0), 0)
+    for d in z_near:
+        i = (1 - d) % 8
+        send(SA.at[pl.ds(((z + d) % NZ) * 16, 16)], R1A.at[i], a1s, a1r.at[i // 4], at_z(d))
+    own_a1 = local(SA.at[pl.ds(z * 16, 16)], R1A.at[1], 0)
 
     def lon_matrix(k, carry):
         edge = k // 4
@@ -240,13 +240,17 @@
                 part = zs[:, half * 128 : half * 128 + 128]
                 other = jnp.where(first, part[128:256], part[256:384])
                 total = part[0:128] + pltpu.roll(other, 64, 1)
-                at = n * 256 + half * 128
-                SM[:, at : at + 128] = (total * inv_lon).astype(BF16)
+                SM[n * 128 : n * 128 + 128, half * 128 : half * 128 + 128] = (total * inv_lon).astype(BF16)
+        down = jnp.dot(SM[128:512], W[0], preferred_element_type=F32)
+        here = jnp.dot(SM[...], W[1], preferred_element_type=F32)
+        up = jnp.dot(SM[0:384], W[2], preferred_element_type=F32)
         for dst in range(4):
-            total = None
-            for src in range(max(0, dst - 1), min(3, dst + 1) + 1):
-                term = jnp.dot(SM[:, src * 256 : src * 256 + 256], W[dst - src + 1], preferred_element_type=F32)
-                total = term if total is None else total + term
+            at = dst * 128
+            total = here[at : at + 128]
+            if dst > 0:
+                total = total + up[at - 128 : at]
+            if dst < 3:
+                total = total + down[at : at + 128]
             total = (total * inv_lat[dst]).astype(BF16)
             for k, lam in enumerate(lams):
                 for half in range(2):
@@ -353,11 +357,12 @@
         wait(FA.at[pl.ds(0, 16)], a4r.at[d])
         zz = (z - d + NZ) % NZ
         home(FA, zz * 16, zz * 16)
+        if d == 4:
+            GA[0:128] = lax.dot_general(MW[0:128], MW[0:128], NT, preferred_element_type=F32)
         wait(FB.at[pl.ds(0, 16)], b4r.at[d])
         yy = (y - d + NY) % NY
         home(FB, yy * 16, 128 + yy * 16)
-    for rows in (slice(0, 128), slice(128, 256)):
-        GA[rows] = lax.dot_general(MW[rows], MW[rows], NT, preferred_element_type=F32)
+    GA[128:256] = lax.dot_general(MW[128:256], MW[128:256], NT, preferred_element_type=F32)
 
     left = GA[0:64] + GA[128:192]
     right = GA[64:128] + GA[192:256]
@@ -438,7 +443,7 @@
         tiles(8, 16), tiles(16, 8),
         tiles(16, 8), tiles(8, 16),
         tiles(2, 4, 8), tiles(2, 4, 8),
-        vmem((256, 1024), BF16), vmem((256, 1024), BF16), vmem((128, 1024), BF16), vmem((128, 1024), BF16),
+        vmem((256, 1024), BF16), vmem((256, 1024), BF16), vmem((128, 1024), BF16), vmem((512, 256), BF16),
         vmem((768, 256), BF16), vmem((384, 128), BF16), vmem((3, 256, 256), BF16),
         tiles(16, 8), tiles(8, 16),
         tiles(16, 8), tiles(8, 16),

time: 86.6 us -> 87.2 us (level)
  no operation moved by 1% of the time
where the time goes in v4:
time: 87.2 us; the launch traced here: 87 us
  Pallas kernels  86.4 us (99%)
    pallas_call x1, Pallas kernels, shards(): pl.pallas_call(kernel, name='coarse_grain', out_shape=(jax.ShapeDtypeStru...  85.4 us

profile of v4, /device:TPU:1, one launch (start us, length us, event | category | flops | bytes accessed | tf_op | source)
XLA Modules:
  0.0 87.0 jit_solution(5735800433202969675)
XLA Ops:
  0.6 85.4 %coarse_grain.1 = (bf16[32,64,256]{2,1,0:T(8,128)(2,1)S(1)}, f32[64,64]{1,0:T(8,128)S(1)}) custom-call(bf16[32,64,256]{2,1,0:T(8,128)(2,1)} %fields.1), custom_call_target="tpu_custom_call" | custom-call | tf_op jit(solution)/shard_map/coarse_grain/pallas_call | solution.py:462
  86.0 1.0 %put_out.1 = (bf16[32,64,256]{2,1,0:T(8,128)(2,1)}, f32[64,64]{1,0:T(8,128)}) custom-call(bf16[32,64,256]{2,1,0:T(8,128)(2,1)S(1)} %get-tuple-element.4.coarse, f32[64,64]{1,0:T(8,128)S(1)} %get-tuple-element.5.gram), custom_call_target="tpu_custom_call" | custom-call | tf_op jit(solution)/shard_map/put_out/pallas_call | solution.py:476
